TPU v7x, 256 devices: a whole 4x4x8 slice. The times are simulated.
256 devices in a mesh: batch: 128 (over y, z, x), tile: 2 (over core).
Axes of the slice: x: 4, y: 4, z: 8, core: 2. Of those that a mesh axis runs over, the one named last changes fastest.
Arguments:
- first_view: bfloat16 [256, 8192], P('batch'), may hold values from -1500 to 1500
- second_view: bfloat16 [256, 8192], P('batch'), may hold values from -1500 to 1500
Outputs:
- grad_first: bfloat16 [256, 8192], P('batch', 'tile')
- grad_second: bfloat16 [256, 8192], P('batch', 'tile')
All inputs are finite; a program needn't handle non-finite values.
Results may differ from a plain program's by a relative error of at most 0.0043.
Values may be sent and summed in bfloat16 or wider, within the bound.
A program may use at most 64 MiB of HBM per device.

v0:
```python
import jax
import jax.numpy as jnp
from jax import lax
from jax.sharding import PartitionSpec as P

BAND = 16


epsilon = 1e-05
decorrelation = 0.0051


def fold_rows(received, row_count, row_groups, group_size, block_width):
    return (
        received.reshape(row_count, row_groups, group_size, block_width)
        .sum(2)
        .reshape(row_count, row_groups * block_width)
    )


def fold_cols(received, row_count, row_groups, group_size, block_width):
    return (
        received.reshape(row_count, row_groups, group_size, block_width)
        .sum(1)
        .reshape(row_count, group_size * block_width)
    )


def per_device(first_view, second_view):
    row_count, feature_width = first_view.shape
    device_count = lax.axis_size("batch")
    band_index = lax.axis_index("batch")
    tile_index = lax.axis_index("tile")
    total_rows = row_count * device_count
    half_width = feature_width // 2
    first_float = first_view.astype(jnp.float32)
    second_float = second_view.astype(jnp.float32)
    moments = lax.psum(
        (
            jnp.sum(first_float, 0),
            jnp.sum(first_float * first_float, 0),
            jnp.sum(second_float, 0),
            jnp.sum(second_float * second_float, 0),
        ),
        "batch",
    )
    mean_first = moments[0] / total_rows
    inverse_first = lax.rsqrt(moments[1] / total_rows - mean_first * mean_first + epsilon)
    mean_second = moments[2] / total_rows
    inverse_second = lax.rsqrt(moments[3] / total_rows - mean_second * mean_second + epsilon)
    norm_first = ((first_float - mean_first) * inverse_first).astype(jnp.bfloat16)
    norm_second = ((second_float - mean_second) * inverse_second).astype(jnp.bfloat16)
    group_size = BAND
    row_groups = device_count // group_size
    block_rows = feature_width * group_size // device_count
    block_cols = feature_width // (2 * group_size)
    row_band = band_index // group_size
    column_block = band_index % group_size + group_size * tile_index
    send_first = jnp.broadcast_to(
        norm_first.reshape(row_count, row_groups, 1, block_rows),
        (row_count, row_groups, group_size, block_rows),
    ).reshape(row_count, device_count * block_rows)
    picked = lax.dynamic_slice_in_dim(
        norm_second.reshape(row_count, 2, group_size, block_cols), tile_index, 1, 1
    )
    send_second = jnp.broadcast_to(picked, (row_count, row_groups, group_size, block_cols)).reshape(
        row_count, device_count * block_cols
    )
    whole_first, whole_second = (
        lax.all_to_all(send_first, "batch", split_axis=1, concat_axis=0, tiled=True),
        lax.all_to_all(send_second, "batch", split_axis=1, concat_axis=0, tiled=True),
    )
    correlation = (
        lax.dot_general(
            whole_first, whole_second, (((0,), (0,)), ((), ())), preferred_element_type=jnp.float32
        )
        / total_rows
    )
    row_ids = row_band * block_rows + lax.iota(jnp.int32, block_rows)
    col_ids = column_block * block_cols + lax.iota(jnp.int32, block_cols)
    on_diagonal = row_ids[:, None] == col_ids[None, :]
    slope_tile = jnp.where(on_diagonal, correlation - 1.0, decorrelation * correlation).astype(
        jnp.bfloat16
    )
    pull_first = lax.dot_general(
        whole_second, slope_tile, (((1,), (1,)), ((), ())), preferred_element_type=jnp.float32
    )
    pull_second = jnp.dot(whole_first, slope_tile, preferred_element_type=jnp.float32)
    half_start = tile_index * half_width
    norm_first_half = lax.dynamic_slice_in_dim(norm_first, half_start, half_width, 1).astype(
        jnp.float32
    )
    norm_second_half = lax.dynamic_slice_in_dim(norm_second, half_start, half_width, 1).astype(
        jnp.float32
    )
    inverse_first_half = lax.dynamic_slice_in_dim(inverse_first, half_start, half_width, 0)
    inverse_second_half = lax.dynamic_slice_in_dim(inverse_second, half_start, half_width, 0)
    back_first, back_second = (
        lax.all_to_all(pull_first, "batch", split_axis=0, concat_axis=1, tiled=True),
        lax.all_to_all(pull_second, "batch", split_axis=0, concat_axis=1, tiled=True),
    )
    full_first = fold_rows(back_first, row_count, row_groups, group_size, block_rows)
    pull_second_half = fold_cols(back_second, row_count, row_groups, group_size, block_cols)
    pull_first_half = lax.psum_scatter(full_first, "tile", scatter_dimension=1, tiled=True)
    column_sums = lax.psum(
        (
            jnp.sum(pull_first_half * norm_first_half, 0, keepdims=True),
            jnp.sum(pull_second_half * norm_second_half, 0, keepdims=True),
        ),
        "batch",
    )
    stat_first = column_sums[0] / total_rows
    stat_second = column_sums[1] / total_rows
    grad_first = (inverse_first_half * (pull_first_half - norm_first_half * stat_first)).astype(
        jnp.bfloat16
    )
    grad_second = (
        inverse_second_half * (pull_second_half - norm_second_half * stat_second)
    ).astype(jnp.bfloat16)
    return (grad_first, grad_second)


def solution(mesh):
    return jax.shard_map(
        per_device,
        mesh=mesh,
        in_specs=(P("batch", None), P("batch", None)),
        out_specs=(P("batch", "tile"), P("batch", "tile")),
        check_vma=False,
    )
```

profile of v0, /device:TPU:0, one launch (start us, length us, event | category | flops | bytes accessed | tf_op | source)
XLA Modules:
  0.0 1036.5 jit_solution(13418832312192321948)
XLA Ops:
  7.2 0.0 all-reduce.4.cloned.1.call-start
  7.2 1.5 convert_reduce_fusion.1
  8.7 1.5 convert_reduce_fusion
  10.3 0.0 all-reduce.4.cloned.1.call-update
  10.3 217.0 %all-reduce.4.cloned.1.call-done = (f32[8192]{0:T(1024)}, f32[8192]{0:T(1024)}, f32[8192]{0:T(1024)}, f32[8192]{0:T(1024)}) async-done(((f32[8192]{0:T(1024)}, f32[8192]{0:T(1024)}, f32[8192]{0:T(1024)}, f32[8192]{0:T(1024)}), (f32[8192]{0:T(1024)}, f32[8192]{0:T(1024)}, f32[8192]{0:T(1024)}, f32[8192]{0:T(1024)})) %all-reduce.4.cloned.1.call-update) | async-done | bytes 131088 | tf_op jit(solution)/shard_map/psum | solution.py:38
  227.3 0.8 broadcast_multiply_fusion
  228.1 0.8 fusion.11
  228.9 0.1 broadcast_in_dim.15
  229.0 1.3 copy.30
  230.3 10.2 all-to-all-start.1
  240.6 0.8 fusion.13
  241.4 14.9 %all-to-all-done.1 = bf16[2,128,1024]{2,0,1:T(2,128)(2,1)S(1)} async-done(((bf16[2,128,1024]{2,0,1:T(2,128)(2,1)}), bf16[2,128,1024]{2,0,1:T(2,128)(2,1)S(1)}, u32[]{:S(2)}, u32[]{:S(2)}) %all-to-all-start.1) | async-done | bytes 524320 | tf_op jit(solution)/shard_map/all_to_all | solution.py:70
  256.3 0.7 broadcast_in_dim.13
  257.1 6.3 all-to-all-start
  263.4 0.5 copy.31
  264.0 11.5 %all-to-all-done = bf16[2,128,256]{2,0,1:T(2,128)(2,1)S(1)} async-done(((bf16[2,128,256]{2,0,1:T(2,128)(2,1)}), bf16[2,128,256]{2,0,1:T(2,128)(2,1)S(1)}, u32[]{:S(2)}, u32[]{:S(2)}) %all-to-all-start) | async-done | bytes 131104 | tf_op jit(solution)/shard_map/all_to_all | solution.py:71
  275.4 0.4 fusion
  275.8 0.3 fusion.4
  276.2 1.8 copy.32
  278.0 6.2 all-to-all-start.2
  284.1 0.3 fusion.1
  284.5 0.9 copy.34
  285.4 22.4 %all-to-all-done.2 = f32[128,2,1024]{2,1,0:T(2,128)S(1)} async-done(((f32[128,2,1024]{2,1,0:T(2,128)}), f32[128,2,1024]{2,1,0:T(2,128)S(1)}, u32[]{:S(2)}, u32[]{:S(2)}) %all-to-all-start.2) | async-done | bytes 1048608 | tf_op jit(solution)/shard_map/all_to_all | solution.py:99
  307.9 7.0 all-to-all-start.3
  314.8 0.0 reduce-scatter.4.cloned.1.call-start
  314.9 0.2 bitcast_reduce_fusion
  315.1 2.6 copy.38
  317.8 0.0 reduce-scatter.4.cloned.1.call-update
  317.8 10.1 all-to-all-done.3
  327.9 0.1 reduce_sum.78
  328.0 0.1 fusion.19
  328.1 9.0 reduce-scatter.4.cloned.1.call-done
  337.0 2.2 copy.39
  339.2 0.1 fusion.15
  339.3 689.0 %all-reduce = (f32[1,4096]{1,0:T(1,128)S(1)}, f32[1,4096]{1,0:T(1,128)S(1)}) all-reduce(f32[1,4096]{1,0:T(1,128)S(1)} %bitcast.62, f32[1,4096]{1,0:T(1,128)S(1)} %bitcast.60), channel_id=1, replica_groups=mesh['batch'=128,'tile'=2] {'batch'}, use_global_device_ids=true, to_apply=%region_11.12 | all-reduce | flops 8192 | bytes 65536 | tf_op jit(solution)/shard_map/psum | solution.py:105
  1028.3 0.6 fusion.18
  1029.0 0.6 fusion.22
  (10 shorter events, 0.1 us)
Async XLA Ops:
  7.2 220.1 %all-reduce.4.cloned.1.call-start = ((), (), s32[]{:S(2)}) async-start(), calls=%async_computation.6 | async-start | bytes 262144 | tf_op jit(solution)/shard_map/psum | solution.py:38
  230.3 26.0 %all-to-all-start.1 = ((bf16[2,128,1024]{2,0,1:T(2,128)(2,1)}), bf16[2,128,1024]{2,0,1:T(2,128)(2,1)S(1)}, u32[]{:S(2)}, u32[]{:S(2)}) async-start(bf16[2,128,1024]{2,0,1:T(2,128)(2,1)} %copy.30), calls=%async_computation.1 | async-start | bytes 1048576 | tf_op jit(solution)/shard_map/all_to_all | solution.py:70
  257.1 18.4 %all-to-all-start = ((bf16[2,128,256]{2,0,1:T(2,128)(2,1)}), bf16[2,128,256]{2,0,1:T(2,128)(2,1)S(1)}, u32[]{:S(2)}, u32[]{:S(2)}) async-start(bf16[2,128,256]{2,0,1:T(2,128)(2,1)} %bitcast.1), calls=%async_computation | async-start | bytes 262144 | tf_op jit(solution)/shard_map/all_to_all | solution.py:71
  278.0 29.9 %all-to-all-start.2 = ((f32[128,2,1024]{2,1,0:T(2,128)}), f32[128,2,1024]{2,1,0:T(2,128)S(1)}, u32[]{:S(2)}, u32[]{:S(2)}) async-start(f32[128,2,1024]{2,1,0:T(2,128)} %copy.32), calls=%async_computation.2 | async-start | bytes 2097152 | tf_op jit(solution)/shard_map/all_to_all | solution.py:99
  307.9 20.1 %all-to-all-start.3 = ((f32[128,2,256]{2,1,0:T(2,128)}), f32[128,2,256]{2,1,0:T(2,128)S(1)}, u32[]{:S(2)}, u32[]{:S(2)}) async-start(f32[128,2,256]{2,1,0:T(2,128)} %copy.34), calls=%async_computation.3 | async-start | bytes 524288 | tf_op jit(solution)/shard_map/all_to_all | solution.py:100
  314.8 22.2 %reduce-scatter.4.cloned.1.call-start = ((), (), s32[]{:S(2)}) async-start(), calls=%async_computation.5 | async-start | bytes 6291456
Sparse Core Ops, SparseCore 0:
  13.7 213.4 all-reduce.3
  318.4 18.5 reduce-scatter.3
where the time goes:
time: 1040 us
  blocking collectives  689 us (66%)
  waiting for transfers between devices  285 us (27%)
  starting transfers between devices  29.8 us (3%)
  between operations  14.3 us (1%)
    psum x1, blocking collectives, per_device(): lax.psum((jnp.sum(pull_first_half * norm_first_half, 0, keepdims=True), j...  689 us
    psum x1, waiting for transfers between devices, per_device(): lax.psum((jnp.sum(first_float, 0), jnp.sum(first_float * first_float, 0),...  217 us
    all_to_all x1, waiting for transfers between devices, per_device(): lax.all_to_all(pull_first, 'batch', split_axis=0, concat_axis=1, tiled=True)  22.4 us
  transfers between devices with their start and end apart: 6, of which 6 were waited for; matrix products, arithmetic and copies ran while one was open for 1% of the time, Pallas kernels for 0%

commit v1 on v0

v1 whole, which is shorter than its diff:
```python
import jax
import jax.numpy as jnp
from jax import lax
from jax.sharding import PartitionSpec as P

BAND = 16


epsilon = 1e-05
decorrelation = 0.0051


def fold_rows(received, row_count, row_groups, group_size, block_width):
    return (
        received.reshape(row_count, row_groups, group_size, block_width)
        .sum(2)
        .reshape(row_count, row_groups * block_width)
    )


def fold_cols(received, row_count, row_groups, group_size, block_width):
    return (
        received.reshape(row_count, row_groups, group_size, block_width)
        .sum(1)
        .reshape(row_count, group_size * block_width)
    )


def normalized(whole, total_rows):
    values = whole.astype(jnp.float32)
    mean_value = jnp.sum(values, 0) / total_rows
    variance = jnp.sum(values * values, 0) / total_rows - mean_value * mean_value
    inverse = lax.rsqrt(variance + epsilon)
    return ((values - mean_value) * inverse).astype(jnp.bfloat16), inverse


def per_device(first_view, second_view):
    row_count, feature_width = first_view.shape
    device_count = lax.axis_size("batch")
    band_index = lax.axis_index("batch")
    tile_index = lax.axis_index("tile")
    total_rows = row_count * device_count
    group_size = BAND
    row_groups = device_count // group_size
    block_rows = feature_width * group_size // device_count
    block_cols = feature_width // (2 * group_size)
    row_band = band_index // group_size
    column_block = band_index % group_size + group_size * tile_index
    send_first = jnp.broadcast_to(
        first_view.reshape(row_count, row_groups, 1, block_rows),
        (row_count, row_groups, group_size, block_rows),
    ).reshape(row_count, device_count * block_rows)
    picked = lax.dynamic_slice_in_dim(
        second_view.reshape(row_count, 2, group_size, block_cols), tile_index, 1, 1
    )
    send_second = jnp.broadcast_to(picked, (row_count, row_groups, group_size, block_cols)).reshape(
        row_count, device_count * block_cols
    )
    whole_first, whole_second = (
        lax.all_to_all(send_first, "batch", split_axis=1, concat_axis=0, tiled=True),
        lax.all_to_all(send_second, "batch", split_axis=1, concat_axis=0, tiled=True),
    )
    norm_first, inverse_first = normalized(whole_first, total_rows)
    norm_second, inverse_second = normalized(whole_second, total_rows)
    correlation = (
        lax.dot_general(
            norm_first, norm_second, (((0,), (0,)), ((), ())), preferred_element_type=jnp.float32
        )
        / total_rows
    )
    row_ids = row_band * block_rows + lax.iota(jnp.int32, block_rows)
    col_ids = column_block * block_cols + lax.iota(jnp.int32, block_cols)
    on_diagonal = row_ids[:, None] == col_ids[None, :]
    slope_tile = jnp.where(on_diagonal, correlation - 1.0, decorrelation * correlation).astype(
        jnp.bfloat16
    )
    weighted = slope_tile.astype(jnp.float32) * correlation
    stat_first = jnp.sum(weighted, 1)
    stat_second = jnp.sum(weighted, 0)
    pull_first = lax.dot_general(
        norm_second, slope_tile, (((1,), (1,)), ((), ())), preferred_element_type=jnp.float32
    )
    pull_second = jnp.dot(norm_first, slope_tile, preferred_element_type=jnp.float32)
    part_first = inverse_first * (pull_first - norm_first.astype(jnp.float32) * stat_first)
    part_second = inverse_second * (pull_second - norm_second.astype(jnp.float32) * stat_second)
    back_first, back_second = (
        lax.all_to_all(part_first, "batch", split_axis=0, concat_axis=1, tiled=True),
        lax.all_to_all(part_second, "batch", split_axis=0, concat_axis=1, tiled=True),
    )
    full_first = fold_rows(back_first, row_count, row_groups, group_size, block_rows)
    grad_second = fold_cols(back_second, row_count, row_groups, group_size, block_cols)
    grad_first = lax.psum_scatter(full_first, "tile", scatter_dimension=1, tiled=True)
    return (grad_first.astype(jnp.bfloat16), grad_second.astype(jnp.bfloat16))


def solution(mesh):
    return jax.shard_map(
        per_device,
        mesh=mesh,
        in_specs=(P("batch", None), P("batch", None)),
        out_specs=(P("batch", "tile"), P("batch", "tile")),
        check_vma=False,
    )
```

time: 1040 us -> 143 us (0.14)
  the two profiles are of different devices: /device:TPU:0 before, /device:TPU:1 now
where the time goes in v1:
time: 143 us; the launch traced here: 142 us
  waiting for transfers between devices  68 us (48%)
  starting transfers between devices  40.7 us (28%)
  between operations  14.2 us (10%)
  local copies, waits for them, and re-layouts  13.5 us (9%)
  other arithmetic  3.18 us (2%)
  matrix products  2.82 us (2%)
    all_to_all x1, waiting for transfers between devices, per_device(): lax.all_to_all(part_first, 'batch', split_axis=0, concat_axis=1, tiled=True)  22.7 us
    all_to_all x1, starting transfers between devices, per_device(): lax.all_to_all(send_second, 'batch', split_axis=1, concat_axis=0, tiled=T...  16.3 us
    all_to_all x1, waiting for transfers between devices, per_device(): lax.all_to_all(send_first, 'batch', split_axis=1, concat_axis=0, tiled=True)  15.2 us
    unnamed x2, waiting for transfers between devices  12.3 us
    all_to_all x1, starting transfers between devices, per_device(): lax.all_to_all(part_second, 'batch', split_axis=0, concat_axis=1, tiled=T...  9.37 us
    all_to_all x1, waiting for transfers between devices, per_device(): lax.all_to_all(part_second, 'batch', split_axis=0, concat_axis=1, tiled=T...  8.99 us
    all_to_all x1, waiting for transfers between devices, per_device(): lax.all_to_all(send_second, 'batch', split_axis=1, concat_axis=0, tiled=T...  8.78 us
    all_to_all x1, starting transfers between devices, per_device(): lax.all_to_all(part_first, 'batch', split_axis=0, concat_axis=1, tiled=True)  8.74 us
  transfers between devices with their start and end apart: 5, of which 5 were waited for; matrix products, arithmetic and copies ran while one was open for 6% of the time, Pallas kernels for 0%

profile of v1, /device:TPU:1, one launch (start us, length us, event | category | flops | bytes accessed | tf_op | source)
XLA Modules:
  0.0 142.4 jit_solution(13058175664994207026)
XLA Ops:
  7.2 0.8 copy.24
  8.0 0.7 broadcast_in_dim.11
  8.7 16.3 %all-to-all-start.1 = ((bf16[2,128,256]{2,0,1:T(2,128)(2,1)}), bf16[2,128,256]{2,0,1:T(2,128)(2,1)S(1)}, u32[]{:S(2)}, u32[]{:S(2)}) async-start(bf16[2,128,256]{2,0,1:T(2,128)(2,1)} %bitcast.2), calls=%async_computation.1 | async-start | bytes 262144 | tf_op jit(solution)/shard_map/all_to_all | solution.py:61
  25.0 0.8 copy.34
  25.8 0.1 broadcast_in_dim.9
  25.9 1.3 copy.17
  27.2 8.8 %all-to-all-done.1 = bf16[2,128,256]{2,0,1:T(2,128)(2,1)S(1)} async-done(((bf16[2,128,256]{2,0,1:T(2,128)(2,1)}), bf16[2,128,256]{2,0,1:T(2,128)(2,1)S(1)}, u32[]{:S(2)}, u32[]{:S(2)}) %all-to-all-start.1) | async-done | bytes 131104 | tf_op jit(solution)/shard_map/all_to_all | solution.py:61
  36.0 6.2 %all-to-all-start = ((bf16[2,128,1024]{2,0,1:T(2,128)(2,1)}), bf16[2,128,1024]{2,0,1:T(2,128)(2,1)S(1)}, u32[]{:S(2)}, u32[]{:S(2)}) async-start(bf16[2,128,1024]{2,0,1:T(2,128)(2,1)} %copy.17), calls=%async_computation | async-start | bytes 1048576 | tf_op jit(solution)/shard_map/all_to_all | solution.py:60
  42.2 0.1 convert_bitcast_fusion.1
  42.3 0.2 reshape.102
  42.5 0.2 convert_reduce_fusion.1
  42.7 0.1 fusion.12
  42.9 15.2 %all-to-all-done = bf16[2,128,1024]{2,0,1:T(2,128)(2,1)S(1)} async-done(((bf16[2,128,1024]{2,0,1:T(2,128)(2,1)}), bf16[2,128,1024]{2,0,1:T(2,128)(2,1)S(1)}, u32[]{:S(2)}, u32[]{:S(2)}) %all-to-all-start) | async-done | bytes 524320 | tf_op jit(solution)/shard_map/all_to_all | solution.py:60
  58.1 0.4 convert_bitcast_fusion
  58.4 0.7 reshape.103
  59.2 0.8 convert_reduce_fusion
  60.0 0.5 fusion.7
  60.6 0.6 fusion.5
  61.2 0.0 copy-start
  61.2 1.0 copy-done
  62.3 0.5 fusion
  62.7 1.6 %all_to_all.48 = f32[128,2,1024]{2,1,0:T(2,128)} reshape(f32[256,1024]{1,0:T(8,128)S(1)} %fusion) | data formatting | bytes 2097152 | tf_op jit(solution)/shard_map/all_to_all | solution.py:87
  64.3 8.7 %all-to-all-start.2 = ((f32[128,2,1024]{2,1,0:T(2,128)}), f32[128,2,1024]{2,1,0:T(2,128)S(1)}, u32[]{:S(2)}, u32[]{:S(2)}) async-start(f32[128,2,1024]{2,1,0:T(2,128)} %all_to_all.48), calls=%async_computation.2 | async-start | bytes 2097152 | tf_op jit(solution)/shard_map/all_to_all | solution.py:87
  73.1 1.7 %fusion.1 = f32[256,256]{1,0:T(8,128)S(1)} fusion(f32[256,1024]{1,0:T(8,128)S(1)} %reshape.103, f32[1024]{0:T(1024)S(1)} %get-tuple-element.8, f32[1024]{0:T(1024)S(1)} %get-tuple-element.9, f32[256]{0:T(256)S(1)} %get-tuple-element.2, f32[256]{0:T(256)S(1)} %get-tuple-element.11, f32[256,256]{1,0:T(8,128)S(1)} %reshape.102, f32[256]{0:T(256)S(1)} %get-tuple-element.10, ...), kind=kOutput, calls=%fused_computation.8 | convolution fusion | flops 137035776 | bytes 2637824 | tf_op jit(solution)/shard_map/dot_general | solution.py:83
  74.8 0.9 all_to_all.51
  75.7 22.7 %all-to-all-done.2 = f32[128,2,1024]{2,1,0:T(2,128)S(1)} async-done(((f32[128,2,1024]{2,1,0:T(2,128)}), f32[128,2,1024]{2,1,0:T(2,128)S(1)}, u32[]{:S(2)}, u32[]{:S(2)}) %all-to-all-start.2) | async-done | bytes 1048608 | tf_op jit(solution)/shard_map/all_to_all | solution.py:87
  98.4 9.4 %all-to-all-start.3 = ((f32[128,2,256]{2,1,0:T(2,128)}), f32[128,2,256]{2,1,0:T(2,128)S(1)}, u32[]{:S(2)}, u32[]{:S(2)}) async-start(f32[128,2,256]{2,1,0:T(2,128)} %all_to_all.51), calls=%async_computation.3 | async-start | bytes 524288 | tf_op jit(solution)/shard_map/all_to_all | solution.py:88
  107.8 0.0 reduce-scatter.4.cloned.1.call-start
  107.8 0.2 bitcast_reduce_fusion
  108.1 2.6 %copy.21 = f32[2,8192]{0,1:T(8,128)} copy(f32[2,8192]{1,0:T(2,128)S(1)} %bitcast.36) | data formatting | bytes 131072
  110.7 0.0 reduce-scatter.4.cloned.1.call-update
  110.7 9.0 %all-to-all-done.3 = f32[128,2,256]{2,1,0:T(2,128)S(1)} async-done(((f32[128,2,256]{2,1,0:T(2,128)}), f32[128,2,256]{2,1,0:T(2,128)S(1)}, u32[]{:S(2)}, u32[]{:S(2)}) %all-to-all-start.3) | async-done | bytes 262176 | tf_op jit(solution)/shard_map/all_to_all | solution.py:88
  119.7 0.7 reduce_sum.79
  120.4 12.3 %reduce-scatter.4.cloned.1.call-done = f32[4096,2]{1,0:T(8,128)} async-done(((f32[8192,2]{1,0:T(8,128)}), f32[4096,2]{1,0:T(8,128)}) %reduce-scatter.4.cloned.1.call-update) | async-done | bytes 32784
  132.7 2.8 %copy.22 = bf16[2,4096]{1,0:T(2,128)(2,1)} copy(f32[2,4096]{0,1:T(8,128)} %bitcast.33) | data formatting | bytes 49152
  (6 shorter events, 0.1 us)
Async XLA Ops:
  8.7 27.3 %all-to-all-start.1 = ((bf16[2,128,256]{2,0,1:T(2,128)(2,1)}), bf16[2,128,256]{2,0,1:T(2,128)(2,1)S(1)}, u32[]{:S(2)}, u32[]{:S(2)}) async-start(bf16[2,128,256]{2,0,1:T(2,128)(2,1)} %bitcast.2), calls=%async_computation.1 | async-start | bytes 262144 | tf_op jit(solution)/shard_map/all_to_all | solution.py:61
  36.0 22.1 %all-to-all-start = ((bf16[2,128,1024]{2,0,1:T(2,128)(2,1)}), bf16[2,128,1024]{2,0,1:T(2,128)(2,1)S(1)}, u32[]{:S(2)}, u32[]{:S(2)}) async-start(bf16[2,128,1024]{2,0,1:T(2,128)(2,1)} %copy.17), calls=%async_computation | async-start | bytes 1048576 | tf_op jit(solution)/shard_map/all_to_all | solution.py:60
  61.2 1.0 copy-start
  64.3 34.0 %all-to-all-start.2 = ((f32[128,2,1024]{2,1,0:T(2,128)}), f32[128,2,1024]{2,1,0:T(2,128)S(1)}, u32[]{:S(2)}, u32[]{:S(2)}) async-start(f32[128,2,1024]{2,1,0:T(2,128)} %all_to_all.48), calls=%async_computation.2 | async-start | bytes 2097152 | tf_op jit(solution)/shard_map/all_to_all | solution.py:87
  98.4 21.3 %all-to-all-start.3 = ((f32[128,2,256]{2,1,0:T(2,128)}), f32[128,2,256]{2,1,0:T(2,128)S(1)}, u32[]{:S(2)}, u32[]{:S(2)}) async-start(f32[128,2,256]{2,1,0:T(2,128)} %all_to_all.51), calls=%async_computation.3 | async-start | bytes 524288 | tf_op jit(solution)/shard_map/all_to_all | solution.py:88
  107.8 24.9 %reduce-scatter.4.cloned.1.call-start = ((), (), s32[]{:S(2)}) async-start(), calls=%async_computation.5 | async-start | bytes 6291456
Sparse Core Ops, SparseCore 0:
  111.2 21.5 reduce-scatter.3
